TPU v7x, 32 devices: a whole 2x2x4 slice. The times are simulated.
32 devices in a mesh: sys: 8 (over z, core), graph: 4 (over y, x).
Axes of the slice: x: 2, y: 2, z: 4, core: 2. Of those that a mesh axis runs over, the one named last changes fastest.
Arguments:
- node_features: bfloat16 [8, 64, 25, 128], P('sys', 'graph'), may hold values from -6 to 6
- atom_slot: int32 [8, 64], P('sys'), may hold values from 0 to 63, each once within a row
- neighbour: int32 [8, 4608], P('sys', 'graph'), may hold values from 0 to 63
- pad_mask: int32 [8, 4608], P('sys', 'graph'), may hold values 0 or 1
- envelope: float32 [8, 4608], P('sys', 'graph'), may hold values from 0.1 to 1
- wigner_rows: bfloat16 [8, 13, 25, 4608], P('sys', None, None, 'graph'), may hold values from -1.1953125 to 1.1953125
- mix_table: float32 [8, 8], replicated, may hold values from 0.1 to 2
- zero_weight: bfloat16 [8, 640, 640], P('sys', 'graph'), may hold values from -0.078125 to 0.078125
- one_weight: bfloat16 [8, 512, 2, 512], P('sys', 'graph'), may hold values from -0.0625 to 0.0625
Outputs:
- update: bfloat16 [8, 64, 25, 128], P('sys', 'graph')
Inputs may be any that keep to these rules, and one draw needn't show every extreme that they name: `neighbour`: atom ids of the edge's own system; edge slots a * 72 to a * 72 + 71 belong to the atom in row a of node_features. `atom_slot`: each system's row names every row of node_features once.
All inputs are finite; a program needn't handle non-finite values. No bound on the sum of `pad_mask` on one device may be relied on, other than what follows from the above.
Results may differ from a plain program's by a relative error of at most 0.025.
Values may be sent and summed in bfloat16 or wider, within the bound.
A program may use at most 64 MiB of HBM per device.

v0:
```python
import math

import jax
import jax.numpy as jnp
from jax import lax
from jax.sharding import PartitionSpec as P

LMAX = 4
NEIGH = 72


def scaled_term(factor, weight):
    term = (factor * weight.astype(jnp.float32)).astype(jnp.bfloat16)
    term = lax.optimization_barrier(term)
    return term.astype(jnp.float32)


def shards(
    node_features,
    atom_slot,
    neighbour,
    pad_mask,
    envelope,
    wigner_rows,
    mix_table,
    zero_weight,
    one_weight,
):
    sys_index = lax.axis_index("sys")
    owned_count = zero_weight.shape[0]
    column = lax.dynamic_slice_in_dim(mix_table, sys_index * owned_count, owned_count, 1).T
    term_zero = jnp.sum(scaled_term(column[:, :, None, None], zero_weight[:, None]), axis=0)
    term_one = jnp.sum(scaled_term(column[:, :, None, None, None], one_weight[:, None]), axis=0)
    summed_zero, summed_one = (
        lax.psum_scatter(
            term_zero.astype(jnp.bfloat16), "sys", scatter_dimension=0, tiled=True
        ).astype(jnp.float32),
        lax.psum_scatter(
            term_one.astype(jnp.bfloat16), "sys", scatter_dimension=0, tiled=True
        ).astype(jnp.float32),
    )
    merged_zero = summed_zero[0]
    merged_one = summed_one[0]
    merged_zero = merged_zero.astype(jnp.bfloat16)
    merged_one = merged_one.astype(jnp.bfloat16)
    features = lax.all_gather(node_features, "graph", axis=1, tiled=True)[0]
    source_rows = jnp.take(atom_slot[0], neighbour[0], axis=0)
    sources = jnp.take(features, source_rows, axis=0)
    frame_local = wigner_rows[0]
    rotated = jnp.einsum(
        "rke,ekc->erc", frame_local, sources, preferred_element_type=jnp.float32
    ).astype(jnp.bfloat16)
    edge_count = rotated.shape[0]
    channels = rotated.shape[2]
    first = rotated[:, : LMAX + 1].reshape(edge_count, -1)
    others = rotated[:, LMAX + 1 :].reshape(edge_count, -1)
    edge_gate = envelope[0] * pad_mask[0].astype(jnp.float32)
    result = lax.dot_general(
        first,
        lax.all_gather(merged_zero, "graph", axis=0, tiled=True),
        (((1,), (1,)), ((), ())),
        preferred_element_type=jnp.float32,
    )
    out_zero = (edge_gate[:, None] * result).astype(jnp.bfloat16)
    segment = lax.all_gather(merged_one, "graph", axis=0, tiled=True)
    real_part = segment[:, 0]
    imag_part = segment[:, 1]
    piece_count = segment.shape[0]
    stacked = jnp.stack(
        [
            jnp.concatenate([real_part, -imag_part], axis=1),
            jnp.concatenate([imag_part, real_part], axis=1),
        ],
        axis=0,
    )
    result = lax.dot_general(
        others,
        stacked.reshape(2 * piece_count, -1),
        (((1,), (1,)), ((), ())),
        preferred_element_type=jnp.float32,
    )
    out_one = (edge_gate[:, None] * result).astype(jnp.bfloat16).reshape(edge_count, 2, piece_count)
    atom_count = edge_count // NEIGH
    harmonics = frame_local.shape[1]
    near_part = jnp.einsum(
        "rkaj,ajrc->akc",
        frame_local[: LMAX + 1].reshape(LMAX + 1, harmonics, atom_count, NEIGH),
        out_zero.reshape(atom_count, NEIGH, LMAX + 1, channels),
        preferred_element_type=jnp.float32,
    )
    far_part = jnp.einsum(
        "rkaj,ajrc->akc",
        frame_local[LMAX + 1 :].reshape(2 * LMAX, harmonics, atom_count, NEIGH),
        out_one.reshape(atom_count, NEIGH, 2 * LMAX, channels),
        preferred_element_type=jnp.float32,
    )
    update = ((near_part + far_part) * (1.0 / math.sqrt(NEIGH))).astype(jnp.bfloat16)
    return update[None]


def solution(mesh):
    return jax.shard_map(
        shards,
        mesh=mesh,
        in_specs=(
            P("sys", "graph", None, None),
            P("sys", None),
            P("sys", "graph"),
            P("sys", "graph"),
            P("sys", "graph"),
            P("sys", None, None, "graph"),
            P(),
            P("sys", "graph", None),
            P("sys", "graph", None, None),
        ),
        out_specs=P("sys", "graph", None, None),
        check_vma=False,
    )
```

profile of v0, /device:TPU:0, one launch (start us, length us, event | category | flops | bytes accessed | tf_op | source)
XLA Modules:
  0.0 141.0 jit_solution(10183846190987760706)
XLA Ops:
  6.5 1.1 bitcast_convert_fusion
  8.0 2.0 %multiply_convert_fusion = bf16[1,8,128,2,512]{4,2,3,1,0:T(8,128)(2,1)} fusion(f32[128,2,512]{2,0,1:T(8,128)S(1)} %copy.32, f32[8]{0:T(128)S(1)} %dynamic-slice_reduce_fusion), kind=kLoop, calls=%fused_computation.7 | loop fusion | flops 2097152 | bytes 2621472 | tf_op jit(solution)/shard_map/convert_element_type | solution.py:13
  10.2 1.6 %multiply_convert_fusion.1 = bf16[1,8,160,640]{3,2,1,0:T(8,128)(2,1)} fusion(f32[160,640]{1,0:T(8,128)S(1)} %bitcast_convert_fusion.1, f32[8]{0:T(128)S(1)} %dynamic-slice_reduce_fusion), kind=kLoop, calls=%fused_computation.10 | loop fusion | flops 1638400 | bytes 2048032 | tf_op jit(solution)/shard_map/convert_element_type | solution.py:13
  11.9 12.9 %all_gather.9 = bf16[1,64,25,128]{3,1,2,0:T(8,128)(2,1)S(1)} all-gather(bf16[1,16,25,128]{3,1,2,0:T(8,128)(2,1)S(1)} %copy-done.8), channel_id=1, replica_groups=mesh['sys'=8,'graph'=4] {'graph'}, dimensions={1}, use_global_device_ids=true | all-gather | bytes 512000 | tf_op jit(solution)/shard_map/all_gather | solution.py:46
  25.1 5.0 %copy.27 = bf16[13,25,1152]{1,0,2:T(8,128)(2,1)} copy(bf16[13,25,1152]{2,0,1:T(8,128)(2,1)S(1)} %bitcast.151) | data formatting | bytes 1497600 | tf_op jit(solution)/shard_map/squeeze | solution.py:49
  32.9 4.3 %fusion.37 = (s32[1152]{0:T(1024)S(1)}, s32[1152,1]{0,1:T(1,128)S(1)}) fusion(s32[]{:T(128)} %bitcast.58, s32[]{:T(128)} %bitcast.59, s32[]{:T(128)} %bitcast.60, s32[]{:T(128)} %bitcast.61, s32[]{:T(128)} %bitcast.62, s32[]{:T(128)} %bitcast.64, s32[]{:T(128)} %bitcast.63, s32[1,1152]{1,0:T(1,128)S(1)} %copy-done.9), kind=kLoop, calls=%fused_computation.106 | loop fusion | flops 17280 | bytes 13852 | tf_op jit(solution)/shard_map/jit(_take)/gather | solution.py:47
  37.2 0.8 compare_reduce_fusion.56
  38.1 35.6 %compare_and_fusion = (pred[1152]{0:T(1024)(128)(4,1)S(1)}, s32[1152]{0:T(1024)S(1)}) fusion(s32[1152]{0:T(1024)S(1)} %reduce.1, pred[1152]{0:T(1024)(128)(4,1)S(1)} %get-tuple-element.61, pred[1152]{0:T(1024)(128)(4,1)S(1)} %get-tuple-element.59, pred[1152]{0:T(1024)(128)(4,1)S(1)} %get-tuple-element.60, pred[1152]{0:T(1024)(128)(4,1)S(1)} %get-tuple-element.58, ...), kind=kLoop, calls=%fused_computation.105 | loop fusion | flops 80640 | bytes 80868 | tf_op jit(solution)/shard_map/jit(_take)/and | solution.py:48
  73.7 6.1 %gather_fusion = bf16[1152,25,128]{2,1,0:T(8,128)(2,1)} fusion(bf16[64,25,128]{2,1,0:T(8,128)(2,1)S(1)} %bitcast.146, s32[2048]{0:T(1024)S(1)} %pad_clamp_fusion), kind=kCustom, calls=%fused_computation | custom fusion | bytes 14750208 | tf_op jit(solution)/shard_map/jit(_take)/gather | solution.py:48
  79.9 7.3 %convert_bitcast_fusion = bf16[1152,13,128]{2,1,0:T(8,128)(2,1)S(1)} fusion(bf16[13,25,1152]{1,0,2:T(8,128)(2,1)} %copy.27, bf16[1152,25,128]{2,1,0:T(8,128)(2,1)} %gather_fusion, pred[1152]{0:T(1024)(128)(4,1)S(1)} %get-tuple-element.62), kind=kOutput, calls=%fused_computation.5 | convolution fusion | flops 101449728 | bytes 11956608 | tf_op jit(solution)/shard_map/rke,ekc->erc/dot_general | solution.py:50
  87.2 1.9 %slice.159 = bf16[1152,8,128]{2,1,0:T(8,128)(2,1)} slice(bf16[1152,13,128]{2,1,0:T(8,128)(2,1)S(1)} %convert_bitcast_fusion), slice={[0:1152], [5:13], [0:128]} | slice | bytes 4718592 | tf_op jit(solution)/shard_map/slice | solution.py:56
  89.3 0.8 slice.21
  90.1 0.9 slice.25
  91.0 2.4 %copy.28 = bf16[1152,5,128]{0,2,1:T(8,128)(2,1)} copy(bf16[1152,5,128]{2,1,0:T(8,128)(2,1)S(1)} %slice.158) | data formatting | bytes 2949120 | tf_op jit(solution)/shard_map/slice | solution.py:55
  93.4 2.8 %reshape.522 = bf16[5,25,16,72]{3,2,0,1:T(8,128)(2,1)} reshape(bf16[1,5,25,1152]{3,1,2,0:T(8,128)(2,1)} %slice.21) | data formatting | bytes 576000 | tf_op jit(solution)/shard_map/reshape | solution.py:87
  96.2 2.4 %copy.39 = bf16[1,8,25,1152]{2,1,3,0:T(8,128)(2,1)S(1)} copy(bf16[1,8,25,1152]{3,1,2,0:T(8,128)(2,1)S(1)} %copy-done.5) | data formatting | bytes 921600 | tf_op jit(solution)/shard_map/reshape | solution.py:93
  98.7 16.5 %all-gather = bf16[1,640,640]{2,1,0:T(8,128)(2,1)S(1)} all-gather(bf16[1,160,640]{2,1,0:T(8,128)(2,1)} %reduce-scatter.3.cloned.1.call-done), channel_id=2, replica_groups=mesh['sys'=8,'graph'=4] {'graph'}, dimensions={1}, use_global_device_ids=true | all-gather | bytes 1024000 | tf_op jit(solution)/shard_map/all_gather | solution.py:60
  115.2 4.1 %fusion.5 = bf16[1152,640]{1,0:T(8,128)(2,1)} fusion(bf16[1152,640]{0,1:T(8,128)(2,1)} %bitcast.156, f32[1152]{0:T(1024)S(1)} %multiply_reduce_fusion, bf16[1,640,640]{2,1,0:T(8,128)(2,1)S(1)} %all-gather), kind=kOutput, calls=%fused_computation.11 | convolution fusion | flops 945192960 | bytes 3772928 | tf_op jit(solution)/shard_map/dot_general | solution.py:58
  119.3 4.4 %reshape.161 = bf16[16,72,5,128]{3,2,1,0:T(8,128)(2,1)} reshape(bf16[1152,640]{1,0:T(8,128)(2,1)} %fusion.5) | data formatting | bytes 2949120 | tf_op jit(solution)/shard_map/reshape | solution.py:88
  123.7 2.1 %fusion.20 = f32[16,128,25]{1,2,0:T(8,128)S(1)} fusion(bf16[16,72,5,128]{3,2,1,0:T(8,128)(2,1)} %reshape.161, bf16[5,25,16,72]{3,2,0,1:T(8,128)(2,1)S(1)} %copy-done.6), kind=kOutput, calls=%fused_computation.21 | convolution fusion | flops 36864000 | bytes 1967360 | tf_op jit(solution)/shard_map/rkaj,ajrc->akc/dot_general | solution.py:85
  125.8 1.4 slice_bitcast_fusion
  127.9 1.5 %copy-done.2 = bf16[1152,8,128]{2,1,0:T(8,128)(2,1)S(1)} copy-done((bf16[1152,8,128]{2,1,0:T(8,128)(2,1)S(1)}, bf16[1152,8,128]{2,1,0:T(8,128)(2,1)}, u32[]{:S(2)}) %copy-start.2) | copy-done | bytes 2359320
  129.4 2.9 %fusion.12 = bf16[144,8,8,128]{3,1,2,0:T(8,128)(2,1)S(1)} fusion(bf16[1024,1024]{1,0:T(8,128)(2,1)S(1)} %bitcast.155, bf16[144,8,8,128]{3,2,1,0:T(8,128)(2,1)S(1)} %bitcast.152, f32[1152]{0:T(1024)S(1)} %multiply_reduce_fusion), kind=kOutput, calls=%fused_computation.17 | convolution fusion | flops 2418278400 | bytes 6820352 | tf_op jit(solution)/shard_map/dot_general | solution.py:76
  132.9 0.9 fusion.32
  (50 shorter events, 6.0 us)
Async XLA Ops:
  6.5 1.3 copy-start
  6.5 73.3 %reduce-scatter.5.cloned.1.call-start = ((), (), s32[]{:S(2)}) async-start(), calls=%async_computation.3 | async-start | bytes 2359296 | tf_op jit(solution)/shard_map/reduce_scatter | solution.py:38
  8.0 2.1 %copy-start.7 = (bf16[1,160,640]{2,1,0:T(8,128)(2,1)S(1)}, bf16[1,160,640]{2,1,0:T(8,128)(2,1)}, u32[]{:S(2)}) copy-start(bf16[1,160,640]{2,1,0:T(8,128)(2,1)} %param.16) | copy-start | bytes 614404
  10.0 1.8 %copy-start.9 = (s32[1,1152]{1,0:T(1,128)S(1)}, s32[1,1152]{1,0:T(1,128)}, u32[]{:S(2)}) copy-start(s32[1,1152]{1,0:T(1,128)} %param.11) | copy-start | bytes 13828
  10.1 1.8 %copy-start.8 = (bf16[1,16,25,128]{3,1,2,0:T(8,128)(2,1)S(1)}, bf16[1,16,25,128]{3,1,2,0:T(8,128)(2,1)}, u32[]{:S(2)}) copy-start(bf16[1,16,25,128]{3,1,2,0:T(8,128)(2,1)} %param.9) | copy-start | bytes 307204
  10.1 88.6 %reduce-scatter.3.cloned.1.call-start = ((), (), s32[]{:S(2)}) async-start(), calls=%async_computation.2 | async-start | bytes 1843200 | tf_op jit(solution)/shard_map/reduce_scatter | solution.py:35
  10.2 14.9 %copy-start.1 = (bf16[1,13,25,1152]{3,1,2,0:T(8,128)(2,1)S(1)}, bf16[1,13,25,1152]{3,1,2,0:T(8,128)(2,1)}, u32[]{:S(2)}) copy-start(bf16[1,13,25,1152]{3,1,2,0:T(8,128)(2,1)} %param.14) | copy-start | bytes 2246404
  11.8 114.0 %all-gather.4.cloned.1.call-start = ((), (), s32[]{:S(2)}) async-start(), calls=%async_computation.4 | async-start | bytes 1310720 | tf_op jit(solution)/shard_map/all_gather | solution.py:65
  25.1 5.0 %copy-start.4 = (s32[1,64]{1,0:T(1,128)S(1)}, s32[1,64]{1,0:T(1,128)}, u32[]{:S(2)}) copy-start(s32[1,64]{1,0:T(1,128)} %param.10) | copy-start | bytes 772
  91.0 5.2 %copy-start.5 = (bf16[1,8,25,1152]{3,1,2,0:T(8,128)(2,1)S(1)}, bf16[1,8,25,1152]{3,1,2,0:T(8,128)(2,1)}, u32[]{:S(2)}) copy-start(bf16[1,8,25,1152]{3,1,2,0:T(8,128)(2,1)} %slice.25) | copy-start | bytes 1382404
  93.4 5.2 %copy-start.10 = (f32[1,1152]{1,0:T(1,128)S(1)}, f32[1,1152]{1,0:T(1,128)}, u32[]{:S(2)}) copy-start(f32[1,1152]{1,0:T(1,128)} %param.13) | copy-start | bytes 13828
  93.4 5.2 %copy-start.11 = (s32[1,1152]{1,0:T(1,128)S(1)}, s32[1,1152]{1,0:T(1,128)}, u32[]{:S(2)}) copy-start(s32[1,1152]{1,0:T(1,128)} %param.12) | copy-start | bytes 13828
  119.3 4.4 %copy-start.6 = (bf16[5,25,16,72]{3,2,0,1:T(8,128)(2,1)S(1)}, bf16[5,25,16,72]{3,2,0,1:T(8,128)(2,1)}, u32[]{:S(2)}) copy-start(bf16[5,25,16,72]{3,2,0,1:T(8,128)(2,1)} %reshape.522) | copy-start | bytes 864004
  125.8 1.5 %copy-start.3 = (bf16[1,512,2,512]{3,1,2,0:T(8,128)(2,1)S(1)}, bf16[1,512,2,512]{3,1,2,0:T(8,128)(2,1)}, u32[]{:S(2)}) copy-start(bf16[1,512,2,512]{3,1,2,0:T(8,128)(2,1)} %all-gather.4.cloned.1.call-done) | copy-start | bytes 3145732
  127.7 1.7 %copy-start.2 = (bf16[1152,8,128]{2,1,0:T(8,128)(2,1)S(1)}, bf16[1152,8,128]{2,1,0:T(8,128)(2,1)}, u32[]{:S(2)}) copy-start(bf16[1152,8,128]{2,1,0:T(8,128)(2,1)} %slice.159) | copy-start | bytes 7077892
Sparse Core Ops, SparseCore 0:
  10.2 38.8 reduce-scatter.4
  51.4 32.7 reduce-scatter.2
  86.0 28.3 all-gather.3
where the time goes:
time: 142 us; the launch traced here: 141 us
  other arithmetic  46.1 us (32%)
  local copies, waits for them, and re-layouts  34.6 us (24%)
  blocking collectives  29.4 us (21%)
  matrix products  17.3 us (12%)
  between operations  13.4 us (9%)
    and x1, other arithmetic, shards(): sources = jnp.take(features, source_rows, axis=0)  35.6 us
    all_gather x1, blocking collectives, shards(): lax.all_gather(merged_zero, 'graph', axis=0, tiled=True)  16.5 us
    all_gather x1, blocking collectives, shards(): features = lax.all_gather(node_features, 'graph', axis=1, tiled=True)[0]  12.9 us
    dot_general x1, matrix products, shards(): jnp.einsum('rke,ekc->erc', frame_local, sources, preferred_element_type=j...  7.33 us
    gather x1, local copies, waits for them, and re-layouts, shards(): sources = jnp.take(features, source_rows, axis=0)  6.11 us
    gather x2, other arithmetic, shards(): source_rows = jnp.take(atom_slot[0], neighbour[0], axis=0)  5.12 us
    squeeze x1, local copies, waits for them, and re-layouts, shards(): frame_local = wigner_rows[0]  4.98 us
    convert_element_type x4, other arithmetic, scaled_term(): term = (factor * weight.astype(jnp.float32)).astype(jnp.bfloat16)  4.78 us
  transfers between devices with their start and end apart: 3, of which 0 were waited for; matrix products, arithmetic and copies ran while one was open for 61% of the time, Pallas kernels for 0%

commit v1 on v0

v1 whole, which is shorter than its diff:
```python
import functools
import math

import jax
import jax.numpy as jnp
from jax import lax
from jax.experimental import pallas as pl
from jax.experimental.pallas import tpu as pltpu
from jax.sharding import PartitionSpec as P

LMAX = 4
NEIGH = 72
CORES = 2
LANES = 128
WIDE = 256
HALVES = 2
MESH = pl.DeviceIdType.MESH


def tree_sum(terms):
    while len(terms) > 1:
        terms = [
            terms[i] + terms[i + 1] if i + 1 < len(terms) else terms[i]
            for i in range(0, len(terms), 2)
        ]
    return terms[0]


def kernel(
    chips,
    peers,
    feat_ref,
    slot_ref,
    near_ref,
    gate_ref,
    frame_ref,
    mix_ref,
    zero_ref,
    one_ref,
    out_ref,
    feats,
    turned,
    chosen,
    picked,
    rows32,
    spread,
    rotated,
    message,
    padded,
    raw_zero,
    raw_one,
    part_zero,
    part_one,
    end_zero,
    end_one,
    map_zero,
    map_one,
    stacked,
    total,
    raw_send,
    raw_recv,
    part_send,
    part_recv,
    feat_send,
    feat_recv,
    map_send,
    map_recv,
):
    experts = chips * CORES
    sys_index = lax.axis_index("sys")
    graph_index = lax.axis_index("graph")
    chip = sys_index // CORES
    core = sys_index % CORES
    up_id = jnp.minimum(sys_index + CORES, experts - 1)
    down_id = jnp.maximum(sys_index - CORES, 0)
    partner_id = chip * CORES + (1 - core)
    last = chips - 1
    is_inner = jnp.logical_and(chip > 0, chip < last)
    is_end = jnp.logical_or(chip == 0, chip == last)

    barrier = pltpu.get_barrier_semaphore()

    def greet(target_sys, target_graph):
        pl.semaphore_signal(
            barrier, inc=1, device_id=(target_sys, target_graph), device_id_type=MESH
        )

    @pl.when(chip < last)
    def _():
        greet(up_id, graph_index)

    @pl.when(chip > 0)
    def _():
        greet(down_id, graph_index)

    greet(partner_id, graph_index)
    for step in range(1, peers):
        greet(sys_index, lax.rem(graph_index + step, peers))
    greeted = (
        peers + jnp.where(chip < last, 1, 0) + jnp.where(chip > 0, 1, 0)
    )
    pl.semaphore_wait(barrier, greeted)

    def own_piece(j):
        return zero_ref if j == 0 else one_ref.at[j - 1]

    def raw_piece(e, j):
        return raw_zero.at[e] if j == 0 else raw_one.at[e, j - 1]

    def raw_copy(e, j, way, source=None):
        target = (up_id, down_id, partner_id)[way]
        return pltpu.make_async_remote_copy(
            src_ref=raw_piece(e, j) if source is None else source,
            dst_ref=raw_piece(e, j),
            send_sem=raw_send.at[way, e, j],
            recv_sem=raw_recv.at[e, j],
            device_id=(target, graph_index),
            device_id_type=MESH,
        )

    goes_up = chip + 1 <= last - 1
    goes_down = chip - 1 >= 1
    pieces = 1 + HALVES

    def feat_copy(step):
        return pltpu.make_async_remote_copy(
            src_ref=feat_ref,
            dst_ref=feats.at[graph_index],
            send_sem=feat_send.at[step],
            recv_sem=feat_recv.at[step],
            device_id=(sys_index, lax.rem(graph_index + step, peers)),
            device_id_type=MESH,
        )

    for step in range(1, peers):
        feat_copy(step).start()

    def each_own(act):
        for j in range(pieces):

            @pl.when(goes_up)
            def _():
                act(raw_copy(sys_index, j, 0, own_piece(j)))

            @pl.when(goes_down)
            def _():
                act(raw_copy(sys_index, j, 1, own_piece(j)))

            act(raw_copy(sys_index, j, 2, own_piece(j)))

    each_own(lambda copy: copy.start())

    def forward(s, j, sent):
        from_low = jnp.logical_and(chip - 1 - s >= 0, chip <= last - 1)
        low = jnp.maximum(chip - 1 - s, 0) * CORES + core
        from_high = jnp.logical_and(chip + 1 + s <= last, chip >= 1)
        high = jnp.minimum(chip + 1 + s, last) * CORES + core

        @pl.when(from_low)
        def _():
            if not sent:
                raw_copy(low, j, 2).wait_recv()

            @pl.when(goes_up)
            def _():
                copy = raw_copy(low, j, 0)
                copy.wait_send() if sent else copy.start()

            copy = raw_copy(low, j, 2)
            copy.wait_send() if sent else copy.start()

        @pl.when(from_high)
        def _():
            if not sent:
                raw_copy(high, j, 2).wait_recv()

            @pl.when(goes_down)
            def _():
                copy = raw_copy(high, j, 1)
                copy.wait_send() if sent else copy.start()

            copy = raw_copy(high, j, 2)
            copy.wait_send() if sent else copy.start()

    atoms = slot_ref.shape[1]
    edges = near_ref.shape[1]
    frames, harmonics = frame_ref.shape[0], frame_ref.shape[1]
    channels = feat_ref.shape[2]
    zero_rows = zero_ref.shape[0]
    one_rows = one_ref.shape[1]
    side = one_ref.shape[2] // 2

    raw_zero[sys_index] = zero_ref[...]
    raw_one[sys_index] = one_ref[...]
    feats[graph_index] = feat_ref[...]
    padded[...] = jnp.zeros_like(padded)
    for r in range(frames):
        padded[r, :harmonics, :] = frame_ref[r]

    by_id = (
        lax.broadcasted_iota(jnp.int32, (atoms, edges), 0) == near_ref[...]
    ).astype(jnp.bfloat16)
    by_slot = (
        lax.broadcasted_iota(jnp.int32, (atoms, atoms), 0) == slot_ref[...]
    ).astype(jnp.bfloat16)
    chosen[...] = jnp.dot(by_slot, by_id, preferred_element_type=jnp.float32).astype(
        jnp.bfloat16
    )

    for step in range(1, peers):
        feat_copy(step).wait_recv()
    for k in range(harmonics):
        block = feats[:, k].reshape(atoms, channels)
        turned[pl.ds(k * channels, channels), :] = block.T

    band = 16

    def rotate_tile(t, carry):
        lanes = pl.ds(pl.multiple_of(t * LANES, LANES), LANES)
        picked[...] = jnp.dot(
            turned[...], chosen[:, lanes], preferred_element_type=jnp.float32
        ).astype(jnp.bfloat16)
        for r in range(frames):
            rows32[r] = frame_ref[r, :, lanes].astype(jnp.float32)

        def widen(r, carry):
            for k in range(harmonics):
                spread[r, k] = jnp.broadcast_to(
                    rows32[r, k : k + 1, :], (band, LANES)
                ).astype(jnp.bfloat16)
            return carry

        lax.fori_loop(0, frames, widen, 0)

        def rotate_band(b, carry):
            start = pl.multiple_of(b * 2 * band, 2 * band)
            held = [
                [
                    picked[pl.ds(k * channels + start + h * band, band), :]
                    for k in range(harmonics)
                ]
                for h in range(2)
            ]
            for r in range(frames):
                weights = [spread[r, k] for k in range(harmonics)]
                for h in range(2):
                    groups = []
                    for low in range(0, harmonics, 5):
                        part = weights[low] * held[h][low]
                        for k in range(low + 1, min(low + 5, harmonics)):
                            part = part + weights[k] * held[h][k]
                        groups.append(part)
                    rotated[pl.ds(r * channels + start + h * band, band), lanes] = tree_sum(
                        groups
                    )
            return carry

        lax.fori_loop(0, channels // (2 * band), rotate_band, 0)
        tiles = edges // LANES
        for j in range(pieces):

            @pl.when(t == min(tiles - 1, (tiles * (j + 1)) // pieces - 1))
            def _():
                forward(0, j, False)

        return carry

    lax.fori_loop(0, edges // LANES, rotate_tile, 0)

    def wait_partner(j):
        for other in range(chips):
            e = other * CORES + (1 - core)

            @pl.when(jnp.logical_or(is_inner, chip == other))
            def _():
                raw_copy(e, j, 2).wait_recv()

    def weighted(get, put, system, members, rows, extra=None):
        step = band if rows % band == 0 else rows

        def body(i, carry):
            at = pl.ds(pl.multiple_of(i * step, step), step)
            acc = None
            for e in members:
                term = mix_ref[system, e] * get(e, at).astype(jnp.float32)
                acc = term if acc is None else acc + term
            if extra is not None:
                acc = acc + extra(at).astype(jnp.float32)
            put(at, acc.astype(jnp.bfloat16))
            return carry

        lax.fori_loop(0, rows // step, body, 0)

    def getter(j):
        if j == 0:
            return lambda e, at: raw_zero[e, at, :]
        return lambda e, at: raw_one[e, j - 1, at, :]

    rows_of = [zero_rows] + [one_rows] * HALVES

    def part_piece(side_index, j):
        return part_zero.at[side_index] if j == 0 else part_one.at[side_index, j - 1]

    def end_piece(j):
        return end_zero if j == 0 else end_one.at[j - 1]

    def part_copy(side_index, j):
        return pltpu.make_async_remote_copy(
            src_ref=part_piece(side_index, j),
            dst_ref=end_piece(j),
            send_sem=part_send.at[side_index, j],
            recv_sem=part_recv.at[j],
            device_id=((down_id, up_id)[side_index], graph_index),
            device_id_type=MESH,
        )

    def map_piece(g, j):
        return map_zero.at[g] if j == 0 else map_one.at[j - 1, g]

    def map_copy(step, j):
        return pltpu.make_async_remote_copy(
            src_ref=map_piece(graph_index, j),
            dst_ref=map_piece(graph_index, j),
            send_sem=map_send.at[step, j],
            recv_sem=map_recv.at[step, j],
            device_id=(sys_index, lax.rem(graph_index + step, peers)),
            device_id_type=MESH,
        )

    def put_map(j):
        ref = map_piece(graph_index, j)

        def put(at, value):
            ref[at, :] = value

        return put

    def put_part(side_index, j):
        ref = part_piece(side_index, j)

        def put(at, value):
            ref[at, :] = value

        return put

    def merge(j):
        for s in range(1, chips - 2):
            forward(s, j, False)
        wait_partner(j)

        @pl.when(chip == 1)
        def _():
            weighted(
                getter(j), put_part(0, j), core, range(CORES, experts), rows_of[j]
            )
            part_copy(0, j).start()

        @pl.when(chip == last - 1)
        def _():
            weighted(
                getter(j),
                put_part(1, j),
                experts - CORES + core,
                range(experts - CORES),
                rows_of[j],
            )
            part_copy(1, j).start()

        @pl.when(is_inner)
        def _():
            weighted(getter(j), put_map(j), sys_index, range(experts), rows_of[j])

        def finish(members):
            part_copy(0, j).wait_recv()
            ref = end_piece(j)
            weighted(
                getter(j),
                put_map(j),
                sys_index,
                members,
                rows_of[j],
                extra=lambda at: ref[at, :],
            )

        @pl.when(chip == 0)
        def _():
            finish(range(CORES))

        @pl.when(chip == last)
        def _():
            finish(range(experts - CORES, experts))

        for step in range(1, peers):
            map_copy(step, j).start()

    def wait_maps(j):
        for step in range(1, peers):
            map_copy(step, j).wait_recv()

    order_zero = (LMAX + 1) * channels
    cuts = [(at, min(WIDE, edges - at)) for at in range(0, edges, WIDE)]

    def apply_zero():
        wait_maps(0)
        for at, width in cuts:
            value = rotated[:order_zero, at : at + width]
            gate = gate_ref[:, at : at + width]
            for g in range(peers):
                y = jnp.dot(map_zero[g], value, preferred_element_type=jnp.float32)
                message[g * zero_rows : (g + 1) * zero_rows, at : at + width] = (
                    gate * y
                ).astype(jnp.bfloat16)

    def apply_one(h):
        wait_maps(1 + h)
        for g in range(peers):
            real = map_one[h, g, :, :side]
            imag = map_one[h, g, :, side:]
            base = 2 * g * one_rows
            stacked[base : base + one_rows, :side] = real
            stacked[base : base + one_rows, side:] = -imag
            stacked[base + one_rows : base + 2 * one_rows, :side] = imag
            stacked[base + one_rows : base + 2 * one_rows, side:] = real
        for at, width in cuts:
            y = jnp.dot(
                stacked[...],
                rotated[order_zero:, at : at + width],
                preferred_element_type=jnp.float32,
            )
            y = (gate_ref[:, at : at + width] * y).astype(jnp.bfloat16)
            for g in range(peers):
                base = 2 * g * one_rows
                to = order_zero + (g * HALVES + h) * one_rows
                message[to : to + one_rows, at : at + width] = y[base : base + one_rows]
                to = to + side
                message[to : to + one_rows, at : at + width] = y[
                    base + one_rows : base + 2 * one_rows
                ]

    merge(0)
    merge(1)
    apply_zero()
    for h in range(1, HALVES):
        merge(1 + h)
        apply_one(h - 1)
    apply_one(HALVES - 1)

    deep = padded.shape[1]
    total[...] = jnp.zeros_like(total)
    for at, width in cuts:
        first = at // NEIGH
        final = (at + width - 1) // NEIGH
        owner = lax.broadcasted_iota(jnp.int32, (deep, width), 1) + at
        masks = [
            jnp.logical_and(owner >= a * NEIGH, owner < (a + 1) * NEIGH)
            for a in range(first, final + 1)
        ]
        columns = []
        for r in range(frames):
            rows = padded[r, :, at : at + width]
            columns.append(
                jnp.concatenate(
                    [jnp.where(mask, rows, jnp.zeros_like(rows)) for mask in masks], axis=0
                )
            )
        left = jnp.concatenate(columns, axis=1)
        right = jnp.concatenate(
            [
                message[r * channels : (r + 1) * channels, at : at + width]
                for r in range(frames)
            ],
            axis=1,
        )
        total[first * deep : (final + 1) * deep, :] += lax.dot_general(
            left, right, (((1,), (1,)), ((), ())), preferred_element_type=jnp.float32
        )
    scale = 1.0 / math.sqrt(NEIGH)
    for a in range(edges // NEIGH):
        out_ref[a] = (total[a * deep : a * deep + harmonics, :] * scale).astype(jnp.bfloat16)

    for step in range(1, peers):
        feat_copy(step).wait_send()
    each_own(lambda copy: copy.wait_send())
    for j in range(pieces):
        for s in range(0, chips - 2):
            forward(s, j, True)

        @pl.when(chip == 1)
        def _():
            part_copy(0, j).wait_send()

        @pl.when(chip == last - 1)
        def _():
            part_copy(1, j).wait_send()

        for step in range(1, peers):
            map_copy(step, j).wait_send()


def shards(
    systems,
    peers,
    node_features,
    atom_slot,
    neighbour,
    pad_mask,
    envelope,
    wigner_rows,
    mix_table,
    zero_weight,
    one_weight,
):
    chips = systems // CORES
    frames, harmonics, edges = wigner_rows.shape[1:]
    own_atoms, _, channels = node_features.shape[1:]
    zero_rows, zero_width = zero_weight.shape[1:]
    one_rows, _, side = one_weight.shape[1:]
    half = one_rows // HALVES
    deep = -(-harmonics // 16) * 16
    bf16, f32 = jnp.bfloat16, jnp.float32
    pieces = 1 + HALVES
    gate = envelope * pad_mask.astype(f32)
    vmem = pl.BlockSpec(memory_space=pltpu.VMEM)
    atoms = atom_slot.shape[1]
    update = pl.pallas_call(
        functools.partial(kernel, chips, peers),
        out_shape=jax.ShapeDtypeStruct((own_atoms, harmonics, channels), bf16),
        in_specs=[vmem] * 5 + [pl.BlockSpec(memory_space=pltpu.SMEM)] + [vmem] * 2,
        out_specs=vmem,
        scratch_shapes=[
            pltpu.VMEM((peers, harmonics, own_atoms, channels), bf16),
            pltpu.VMEM((harmonics * channels, atoms), bf16),
            pltpu.VMEM((atoms, edges), bf16),
            pltpu.VMEM((harmonics * channels, LANES), bf16),
            pltpu.VMEM((frames, harmonics, LANES), f32),
            pltpu.VMEM((frames, harmonics, 16, LANES), bf16),
            pltpu.VMEM((frames * channels, edges), bf16),
            pltpu.VMEM((frames * channels, edges), bf16),
            pltpu.VMEM((frames, deep, edges), bf16),
            pltpu.VMEM((systems, zero_rows, zero_width), bf16),
            pltpu.VMEM((systems, HALVES, half, 2 * side), bf16),
            pltpu.VMEM((2, zero_rows, zero_width), bf16),
            pltpu.VMEM((2, HALVES, half, 2 * side), bf16),
            pltpu.VMEM((zero_rows, zero_width), bf16),
            pltpu.VMEM((HALVES, half, 2 * side), bf16),
            pltpu.VMEM((peers, zero_rows, zero_width), bf16),
            pltpu.VMEM((HALVES, peers, half, 2 * side), bf16),
            pltpu.VMEM((2 * peers * half, 2 * side), bf16),
            pltpu.VMEM((own_atoms * deep, channels), f32),
            pltpu.SemaphoreType.DMA((3, systems, pieces)),
            pltpu.SemaphoreType.DMA((systems, pieces)),
            pltpu.SemaphoreType.DMA((2, pieces)),
            pltpu.SemaphoreType.DMA((pieces,)),
            pltpu.SemaphoreType.DMA((peers,)),
            pltpu.SemaphoreType.DMA((peers,)),
            pltpu.SemaphoreType.DMA((peers, pieces)),
            pltpu.SemaphoreType.DMA((peers, pieces)),
        ],
        compiler_params=pltpu.CompilerParams(
            collective_id=0, has_side_effects=True, vmem_limit_bytes=60 * 1024 * 1024
        ),
        name="edge_convolution",
    )(
        jnp.transpose(node_features[0], (1, 0, 2)),
        atom_slot,
        neighbour,
        gate,
        wigner_rows[0],
        mix_table,
        zero_weight[0],
        one_weight[0].reshape(HALVES, half, 2 * side),
    )
    return update[None]


def solution(mesh):
    return jax.shard_map(
        functools.partial(shards, mesh.shape["sys"], mesh.shape["graph"]),
        mesh=mesh,
        in_specs=(
            P("sys", "graph", None, None),
            P("sys", None),
            P("sys", "graph"),
            P("sys", "graph"),
            P("sys", "graph"),
            P("sys", None, None, "graph"),
            P(),
            P("sys", "graph", None),
            P("sys", "graph", None, None),
        ),
        out_specs=P("sys", "graph", None, None),
        check_vma=False,
    )
```

time: 142 us -> 80.9 us (0.57)
  Pallas kernels: 0 us -> 73.7 us
  other arithmetic: 46.1 us -> 1.3 us
  blocking collectives: 29.4 us -> 0 us
  local copies, waits for them, and re-layouts: 34.6 us -> 5.67 us
  matrix products: 17.3 us -> 0 us
  between operations: 13.4 us -> 0.01 us
    pallas_call x0 -> x1, Pallas kernels: none -> 73.7 us  [shards(): pl.pallas_call(functools.partial(kernel, chips, peers), out_shape=jax.Sha...]
    and x1 -> x0, other arithmetic: 35.6 us -> none  [shards(): sources = jnp.take(features, source_rows, axis=0)]
    all_gather x2 -> x0, blocking collectives: 29.4 us -> none  [the longest x1 16.5 us: shards(): lax.all_gather(merged_zero, 'graph', axis=0, tiled=True)]
    dot_general x5 -> x0, matrix products: 17.3 us -> none  [the longest x1 7.33 us: shards(): jnp.einsum('rke,ekc->erc', frame_local, sources, preferred_element_type=j...]
    reshape x3 -> x0, local copies, waits for them, and re-layouts: 9.55 us -> none  [the longest x1 4.36 us: shards(): out_zero.reshape(atom_count, NEIGH, LMAX + 1, channels)]
    gather x5 -> x0, local copies, waits for them, and re-layouts: 8.97 us -> none  [the longest x1 6.11 us: shards(): sources = jnp.take(features, source_rows, axis=0)]
    squeeze x2 -> x0, local copies, waits for them, and re-layouts: 6.33 us -> none  [the longest x1 4.98 us: shards(): frame_local = wigner_rows[0]]
    slice x5 -> x0, local copies, waits for them, and re-layouts: 6.15 us -> none  [the longest x2 2.57 us: shards(): first = rotated[:, :LMAX + 1].reshape(edge_count, -1)]
  transfers between devices with their start and end apart: 3 -> 0, of which waited for: 0 -> 0; matrix products, arithmetic and copies ran while one was open for 61% -> 0% of each run, Pallas kernels for 0% -> 0%
where the time goes in v1:
time: 80.9 us; the launch traced here: 80.7 us
  Pallas kernels  73.7 us (91%)
  local copies, waits for them, and re-layouts  5.67 us (7%)
  other arithmetic  1.3 us (2%)
    pallas_call x1, Pallas kernels, shards(): pl.pallas_call(functools.partial(kernel, chips, peers), out_shape=jax.Sha...  73.7 us
    unnamed x1, local copies, waits for them, and re-layouts  2.27 us
    another operation x1, local copies, waits for them, and re-layouts, shards(): one_weight[0].reshape(HALVES, half, 2 * side)  1.81 us

profile of v1, /device:TPU:0, one launch (start us, length us, event | category | flops | bytes accessed | tf_op | source)
XLA Modules:
  0.0 80.7 jit_solution(7542128293171319759)
XLA Ops:
  0.0 1.3 %convert_multiply_fusion.gate_ref = f32[1,1152]{1,0:T(1,128)} fusion(f32[1,1152]{1,0:T(1,128)} %param.13, s32[1,1152]{1,0:T(1,128)} %param.12), kind=kLoop, calls=%fused_computation.1 | loop fusion | flops 2304 | bytes 13824 | tf_op jit(solution)/shard_map/mul | solution.py:522
  1.3 1.8 %reshape_squeeze.3.one_ref = bf16[2,64,1024]{2,1,0:T(8,128)(2,1)} reshape(bf16[1,128,2,512]{3,2,1,0:T(2,128)(2,1)} %param.17) | data formatting | bytes 524288 | tf_op jit(solution)/shard_map/reshape;squeeze | solution.py:571
  3.1 2.3 %copy.13 = bf16[1,13,25,1152]{3,2,1,0:T(8,128)(2,1)} copy(bf16[1,13,25,1152]{3,1,2,0:T(8,128)(2,1)} %param.14) | data formatting | bytes 1497600 | tf_op args[5]
  5.4 73.7 %edge_convolution.1 = bf16[16,25,128]{2,1,0:T(8,128)(2,1)} custom-call(bf16[25,16,128]{2,1,0:T(8,128)(2,1)} %bitcast.11, s32[1,64]{1,0:T(1,128)} %slot_ref.1, s32[1,1152]{1,0:T(1,128)} %near_ref.1, f32[1,1152]{1,0:T(1,128)} %convert_multiply_fusion.gate_ref, bf16[13,25,1152]{2,1,0:T(8,128)(2,1)} %bitcast.8, f32[8,8]{1,0:T(8,128)} %mix_ref.1, ...), custom_call_target="tpu_custom_call" | custom-call | tf_op jit(solution)/shard_map/edge_convolution/pallas_call | solution.py:525
  79.1 1.6 %copy.11 = bf16[1,16,25,128]{3,1,2,0:T(8,128)(2,1)} copy(bf16[1,16,25,128]{3,2,1,0:T(8,128)(2,1)} %bitcast.9) | data formatting | bytes 204800 | tf_op jit(solution)/shard_map/broadcast_in_dim | solution.py:573

commit v2 on v1

--- a/solution.py
+++ b/solution.py
@@ -13,7 +13,8 @@
 CORES = 2
 LANES = 128
 WIDE = 256
-HALVES = 2
+ZERO_PARTS = 2
+ONE_PARTS = 4
 MESH = pl.DeviceIdType.MESH
 
 
@@ -32,7 +33,8 @@
     feat_ref,
     slot_ref,
     near_ref,
-    gate_ref,
+    mask_ref,
+    envelope_ref,
     frame_ref,
     mix_ref,
     zero_ref,
@@ -41,6 +43,8 @@
     feats,
     turned,
     chosen,
+    pair,
+    gate_ref,
     picked,
     rows32,
     spread,
@@ -102,10 +106,10 @@
     pl.semaphore_wait(barrier, greeted)
 
     def own_piece(j):
-        return zero_ref if j == 0 else one_ref.at[j - 1]
+        return zero_ref.at[j] if j < ZERO_PARTS else raw_piece(sys_index, j)
 
     def raw_piece(e, j):
-        return raw_zero.at[e] if j == 0 else raw_one.at[e, j - 1]
+        return raw_zero.at[e, j] if j < ZERO_PARTS else raw_one.at[e, j - ZERO_PARTS]
 
     def raw_copy(e, j, way, source=None):
         target = (up_id, down_id, partner_id)[way]
@@ -120,7 +124,7 @@
 
     goes_up = chip + 1 <= last - 1
     goes_down = chip - 1 >= 1
-    pieces = 1 + HALVES
+    pieces = ZERO_PARTS + ONE_PARTS
 
     def feat_copy(step):
         return pltpu.make_async_remote_copy(
@@ -135,20 +139,22 @@
     for step in range(1, peers):
         feat_copy(step).start()
 
-    def each_own(act):
-        for j in range(pieces):
-
-            @pl.when(goes_up)
-            def _():
-                act(raw_copy(sys_index, j, 0, own_piece(j)))
-
-            @pl.when(goes_down)
-            def _():
-                act(raw_copy(sys_index, j, 1, own_piece(j)))
-
-            act(raw_copy(sys_index, j, 2, own_piece(j)))
-
-    each_own(lambda copy: copy.start())
+    def send_own(j, act):
+        @pl.when(goes_up)
+        def _():
+            act(raw_copy(sys_index, j, 0, own_piece(j)))
+
+        @pl.when(goes_down)
+        def _():
+            act(raw_copy(sys_index, j, 1, own_piece(j)))
+
+        act(raw_copy(sys_index, j, 2, own_piece(j)))
+
+    def start(copy):
+        copy.start()
+
+    for j in range(ZERO_PARTS):
+        send_own(j, start)
 
     def forward(s, j, sent):
         from_low = jnp.logical_and(chip - 1 - s >= 0, chip <= last - 1)
@@ -184,19 +190,28 @@
 
     atoms = slot_ref.shape[1]
     edges = near_ref.shape[1]
-    frames, harmonics = frame_ref.shape[0], frame_ref.shape[1]
+    harmonics, frames = frame_ref.shape[0], frame_ref.shape[1]
     channels = feat_ref.shape[2]
-    zero_rows = zero_ref.shape[0]
-    one_rows = one_ref.shape[1]
-    side = one_ref.shape[2] // 2
+    zero_rows = zero_ref.shape[1]
+    one_rows = one_ref.shape[0] // ONE_PARTS
+    side = one_ref.shape[2]
+
+    pair[...] = one_ref[...].astype(jnp.float32)
+    for q in range(ONE_PARTS):
+        for part in range(2):
+            raw_one[sys_index, q, :, part * side : (part + 1) * side] = pair[
+                q * one_rows : (q + 1) * one_rows, part, :
+            ].astype(jnp.bfloat16)
+
+    @pl.when(is_end)
+    def _():
+        for j in range(ZERO_PARTS, pieces):
+            send_own(j, start)
 
     raw_zero[sys_index] = zero_ref[...]
-    raw_one[sys_index] = one_ref[...]
     feats[graph_index] = feat_ref[...]
+    gate_ref[...] = envelope_ref[...] * mask_ref[...].astype(jnp.float32)
     padded[...] = jnp.zeros_like(padded)
-    for r in range(frames):
-        padded[r, :harmonics, :] = frame_ref[r]
-
     by_id = (
         lax.broadcasted_iota(jnp.int32, (atoms, edges), 0) == near_ref[...]
     ).astype(jnp.bfloat16)
@@ -220,23 +235,25 @@
         picked[...] = jnp.dot(
             turned[...], chosen[:, lanes], preferred_element_type=jnp.float32
         ).astype(jnp.bfloat16)
+        for k in range(harmonics):
+            rows32[k] = frame_ref[k, :, lanes].astype(jnp.float32)
         for r in range(frames):
-            rows32[r] = frame_ref[r, :, lanes].astype(jnp.float32)
-
-        def widen(r, carry):
-            for k in range(harmonics):
+            padded[r, :harmonics, lanes] = rows32[:, r, :].astype(jnp.bfloat16)
+
+        def widen(k, carry):
+            for r in range(frames):
                 spread[r, k] = jnp.broadcast_to(
-                    rows32[r, k : k + 1, :], (band, LANES)
+                    rows32[k, r : r + 1, :], (band, LANES)
                 ).astype(jnp.bfloat16)
             return carry
 
-        lax.fori_loop(0, frames, widen, 0)
+        lax.fori_loop(0, harmonics, widen, 0)
 
         def rotate_band(b, carry):
-            start = pl.multiple_of(b * 2 * band, 2 * band)
+            begin = pl.multiple_of(b * 2 * band, 2 * band)
             held = [
                 [
-                    picked[pl.ds(k * channels + start + h * band, band), :]
+                    picked[pl.ds(k * channels + begin + h * band, band), :]
                     for k in range(harmonics)
                 ]
                 for h in range(2)
@@ -250,22 +267,19 @@
                         for k in range(low + 1, min(low + 5, harmonics)):
                             part = part + weights[k] * held[h][k]
                         groups.append(part)
-                    rotated[pl.ds(r * channels + start + h * band, band), lanes] = tree_sum(
+                    rotated[pl.ds(r * channels + begin + h * band, band), lanes] = tree_sum(
                         groups
                     )
             return carry
 
         lax.fori_loop(0, channels // (2 * band), rotate_band, 0)
-        tiles = edges // LANES
-        for j in range(pieces):
-
-            @pl.when(t == min(tiles - 1, (tiles * (j + 1)) // pieces - 1))
+        for name, j, tile in plan:
+
+            @pl.when(t == tile)
             def _():
-                forward(0, j, False)
+                first_leg(j) if name == "leg" else merge(j)
 
         return carry
-
-    lax.fori_loop(0, edges // LANES, rotate_tile, 0)
 
     def wait_partner(j):
         for other in range(chips):
@@ -292,17 +306,19 @@
         lax.fori_loop(0, rows // step, body, 0)
 
     def getter(j):
-        if j == 0:
-            return lambda e, at: raw_zero[e, at, :]
-        return lambda e, at: raw_one[e, j - 1, at, :]
-
-    rows_of = [zero_rows] + [one_rows] * HALVES
+        if j < ZERO_PARTS:
+            return lambda e, at: raw_zero[e, j, at, :]
+        return lambda e, at: raw_one[e, j - ZERO_PARTS, at, :]
+
+    rows_of = [zero_rows] * ZERO_PARTS + [one_rows] * ONE_PARTS
 
     def part_piece(side_index, j):
-        return part_zero.at[side_index] if j == 0 else part_one.at[side_index, j - 1]
+        if j < ZERO_PARTS:
+            return part_zero.at[side_index, j]
+        return part_one.at[side_index, j - ZERO_PARTS]
 
     def end_piece(j):
-        return end_zero if j == 0 else end_one.at[j - 1]
+        return end_zero.at[j] if j < ZERO_PARTS else end_one.at[j - ZERO_PARTS]
 
     def part_copy(side_index, j):
         return pltpu.make_async_remote_copy(
@@ -315,7 +331,7 @@
         )
 
     def map_piece(g, j):
-        return map_zero.at[g] if j == 0 else map_one.at[j - 1, g]
+        return map_zero.at[j, g] if j < ZERO_PARTS else map_one.at[j - ZERO_PARTS, g]
 
     def map_copy(step, j):
         return pltpu.make_async_remote_copy(
@@ -342,6 +358,14 @@
             ref[at, :] = value
 
         return put
+
+    def first_leg(j):
+        forward(0, j, False)
+        if j + ZERO_PARTS < pieces:
+
+            @pl.when(is_inner)
+            def _():
+                send_own(j + ZERO_PARTS, start)
 
     def merge(j):
         for s in range(1, chips - 2):
@@ -401,26 +425,35 @@
     cuts = [(at, min(WIDE, edges - at)) for at in range(0, edges, WIDE)]
 
     def apply_zero():
-        wait_maps(0)
+        for j in range(ZERO_PARTS):
+            wait_maps(j)
         for at, width in cuts:
-            value = rotated[:order_zero, at : at + width]
-            gate = gate_ref[:, at : at + width]
+            y = jnp.dot(
+                map_zero[...].reshape(ZERO_PARTS * peers * zero_rows, order_zero),
+                rotated[:order_zero, at : at + width],
+                preferred_element_type=jnp.float32,
+            )
+            y = (gate_ref[:, at : at + width] * y).astype(jnp.bfloat16)
+            for j in range(ZERO_PARTS):
+                for g in range(peers):
+                    base = (j * peers + g) * zero_rows
+                    to = (g * ZERO_PARTS + j) * zero_rows
+                    message[to : to + zero_rows, at : at + width] = y[base : base + zero_rows]
+
+    group = 2
+    whole = group * peers * one_rows
+
+    def apply_one(h):
+        for q in range(group):
+            wait_maps(ZERO_PARTS + h + q)
             for g in range(peers):
-                y = jnp.dot(map_zero[g], value, preferred_element_type=jnp.float32)
-                message[g * zero_rows : (g + 1) * zero_rows, at : at + width] = (
-                    gate * y
-                ).astype(jnp.bfloat16)
-
-    def apply_one(h):
-        wait_maps(1 + h)
-        for g in range(peers):
-            real = map_one[h, g, :, :side]
-            imag = map_one[h, g, :, side:]
-            base = 2 * g * one_rows
-            stacked[base : base + one_rows, :side] = real
-            stacked[base : base + one_rows, side:] = -imag
-            stacked[base + one_rows : base + 2 * one_rows, :side] = imag
-            stacked[base + one_rows : base + 2 * one_rows, side:] = real
+                real = map_one[h + q, g, :, :side]
+                imag = map_one[h + q, g, :, side:]
+                base = (q * peers + g) * one_rows
+                stacked[base : base + one_rows, :side] = real
+                stacked[base : base + one_rows, side:] = -imag
+                stacked[whole + base : whole + base + one_rows, :side] = imag
+                stacked[whole + base : whole + base + one_rows, side:] = real
         for at, width in cuts:
             y = jnp.dot(
                 stacked[...],
@@ -428,22 +461,33 @@
                 preferred_element_type=jnp.float32,
             )
             y = (gate_ref[:, at : at + width] * y).astype(jnp.bfloat16)
-            for g in range(peers):
-                base = 2 * g * one_rows
-                to = order_zero + (g * HALVES + h) * one_rows
-                message[to : to + one_rows, at : at + width] = y[base : base + one_rows]
-                to = to + side
-                message[to : to + one_rows, at : at + width] = y[
-                    base + one_rows : base + 2 * one_rows
-                ]
-
-    merge(0)
-    merge(1)
+            for q in range(group):
+                for g in range(peers):
+                    base = (q * peers + g) * one_rows
+                    to = order_zero + (g * ONE_PARTS + h + q) * one_rows
+                    message[to : to + one_rows, at : at + width] = y[base : base + one_rows]
+                    to = to + side
+                    base = base + whole
+                    message[to : to + one_rows, at : at + width] = y[base : base + one_rows]
+
+    tiles = edges // LANES
+    order = []
+    for j in range(pieces):
+        order.append(("leg", j))
+        if j >= 1:
+            order.append(("merge", j - 1))
+    order.append(("merge", pieces - 1))
+    late = 2
+    plan = [
+        (name, j, min(tiles - 1, ((place + 1) * tiles) // (len(order) - late)))
+        for place, (name, j) in enumerate(order[:-late])
+    ]
+    lax.fori_loop(0, tiles, rotate_tile, 0)
+    merge(pieces - 2)
     apply_zero()
-    for h in range(1, HALVES):
-        merge(1 + h)
-        apply_one(h - 1)
-    apply_one(HALVES - 1)
+    merge(pieces - 1)
+    for h in range(0, ONE_PARTS, group):
+        apply_one(h)
 
     deep = padded.shape[1]
     total[...] = jnp.zeros_like(total)
@@ -471,17 +515,18 @@
             ],
             axis=1,
         )
-        total[first * deep : (final + 1) * deep, :] += lax.dot_general(
+        product = lax.dot_general(
             left, right, (((1,), (1,)), ((), ())), preferred_element_type=jnp.float32
         )
+        total[first : final + 1] += product.reshape(final + 1 - first, deep, channels)
     scale = 1.0 / math.sqrt(NEIGH)
-    for a in range(edges // NEIGH):
-        out_ref[a] = (total[a * deep : a * deep + harmonics, :] * scale).astype(jnp.bfloat16)
+    for k in range(harmonics):
+        out_ref[k] = (total[:, k, :] * scale).astype(jnp.bfloat16)
 
     for step in range(1, peers):
         feat_copy(step).wait_send()
-    each_own(lambda copy: copy.wait_send())
     for j in range(pieces):
+        send_own(j, lambda copy: copy.wait_send())
         for s in range(0, chips - 2):
             forward(s, j, True)
 
@@ -515,38 +560,40 @@
     own_atoms, _, channels = node_features.shape[1:]
     zero_rows, zero_width = zero_weight.shape[1:]
     one_rows, _, side = one_weight.shape[1:]
-    half = one_rows // HALVES
+    half = one_rows // ONE_PARTS
+    share = zero_rows // ZERO_PARTS
     deep = -(-harmonics // 16) * 16
     bf16, f32 = jnp.bfloat16, jnp.float32
-    pieces = 1 + HALVES
-    gate = envelope * pad_mask.astype(f32)
+    pieces = ZERO_PARTS + ONE_PARTS
     vmem = pl.BlockSpec(memory_space=pltpu.VMEM)
     atoms = atom_slot.shape[1]
     update = pl.pallas_call(
         functools.partial(kernel, chips, peers),
-        out_shape=jax.ShapeDtypeStruct((own_atoms, harmonics, channels), bf16),
-        in_specs=[vmem] * 5 + [pl.BlockSpec(memory_space=pltpu.SMEM)] + [vmem] * 2,
+        out_shape=jax.ShapeDtypeStruct((harmonics, own_atoms, channels), bf16),
+        in_specs=[vmem] * 6 + [pl.BlockSpec(memory_space=pltpu.SMEM)] + [vmem] * 2,
         out_specs=vmem,
         scratch_shapes=[
             pltpu.VMEM((peers, harmonics, own_atoms, channels), bf16),
             pltpu.VMEM((harmonics * channels, atoms), bf16),
             pltpu.VMEM((atoms, edges), bf16),
+            pltpu.VMEM((one_rows, 2, side), f32),
+            pltpu.VMEM((1, edges), f32),
             pltpu.VMEM((harmonics * channels, LANES), bf16),
-            pltpu.VMEM((frames, harmonics, LANES), f32),
+            pltpu.VMEM((harmonics, frames, LANES), f32),
             pltpu.VMEM((frames, harmonics, 16, LANES), bf16),
             pltpu.VMEM((frames * channels, edges), bf16),
             pltpu.VMEM((frames * channels, edges), bf16),
             pltpu.VMEM((frames, deep, edges), bf16),
-            pltpu.VMEM((systems, zero_rows, zero_width), bf16),
-            pltpu.VMEM((systems, HALVES, half, 2 * side), bf16),
-            pltpu.VMEM((2, zero_rows, zero_width), bf16),
-            pltpu.VMEM((2, HALVES, half, 2 * side), bf16),
-            pltpu.VMEM((zero_rows, zero_width), bf16),
-            pltpu.VMEM((HALVES, half, 2 * side), bf16),
-            pltpu.VMEM((peers, zero_rows, zero_width), bf16),
-            pltpu.VMEM((HALVES, peers, half, 2 * side), bf16),
-            pltpu.VMEM((2 * peers * half, 2 * side), bf16),
-            pltpu.VMEM((own_atoms * deep, channels), f32),
+            pltpu.VMEM((systems, ZERO_PARTS, share, zero_width), bf16),
+            pltpu.VMEM((systems, ONE_PARTS, half, 2 * side), bf16),
+            pltpu.VMEM((2, ZERO_PARTS, share, zero_width), bf16),
+            pltpu.VMEM((2, ONE_PARTS, half, 2 * side), bf16),
+            pltpu.VMEM((ZERO_PARTS, share, zero_width), bf16),
+            pltpu.VMEM((ONE_PARTS, half, 2 * side), bf16),
+            pltpu.VMEM((ZERO_PARTS, peers, share, zero_width), bf16),
+            pltpu.VMEM((ONE_PARTS, peers, half, 2 * side), bf16),
+            pltpu.VMEM((4 * peers * half, 2 * side), bf16),
+            pltpu.VMEM((own_atoms, deep, channels), f32),
             pltpu.SemaphoreType.DMA((3, systems, pieces)),
             pltpu.SemaphoreType.DMA((systems, pieces)),
             pltpu.SemaphoreType.DMA((2, pieces)),
@@ -564,13 +611,14 @@
         jnp.transpose(node_features[0], (1, 0, 2)),
         atom_slot,
         neighbour,
-        gate,
-        wigner_rows[0],
+        pad_mask,
+        envelope,
+        jnp.transpose(wigner_rows[0], (1, 0, 2)),
         mix_table,
-        zero_weight[0],
-        one_weight[0].reshape(HALVES, half, 2 * side),
+        zero_weight[0].reshape(ZERO_PARTS, share, zero_width),
+        one_weight[0],
     )
-    return update[None]
+    return jnp.transpose(update, (1, 0, 2))[None]
 
 
 def solution(mesh):

time: 80.9 us -> 66.4 us (0.82)
  Pallas kernels: 73.7 us -> 64.6 us
  local copies, waits for them, and re-layouts: 5.67 us -> 1.54 us
  other arithmetic: 1.3 us -> 0 us
    pallas_call x1, Pallas kernels: 73.7 us -> 64.6 us  [shards(): pl.pallas_call(functools.partial(kernel, chips, peers), out_shape=jax.Sha...]
    another operation x1 -> x0, local copies, waits for them, and re-layouts: 1.81 us -> none  [shards(): one_weight[0].reshape(HALVES, half, 2 * side)]
    broadcast_in_dim x1 -> x0, local copies, waits for them, and re-layouts: 1.59 us -> none  [shards(): return update[None]]
    mul x1 -> x0, other arithmetic: 1.3 us -> none  [shards(): gate = envelope * pad_mask.astype(f32)]
where the time goes in v2:
time: 66.4 us; the launch traced here: 66.2 us
  Pallas kernels  64.6 us (97%)
  local copies, waits for them, and re-layouts  1.54 us (2%)
    pallas_call x1, Pallas kernels, shards(): pl.pallas_call(functools.partial(kernel, chips, peers), out_shape=jax.Sha...  64.6 us
    unnamed x1, local copies, waits for them, and re-layouts  1.54 us

profile of v2, /device:TPU:0, one launch (start us, length us, event | category | flops | bytes accessed | tf_op | source)
XLA Modules:
  0.0 66.2 jit_solution(17271750197670049671)
XLA Ops:
  0.0 64.6 %edge_convolution.1 = bf16[25,16,128]{2,1,0:T(8,128)(2,1)} custom-call(bf16[25,16,128]{2,1,0:T(8,128)(2,1)} %bitcast.15, s32[1,64]{1,0:T(1,128)} %slot_ref.1, s32[1,1152]{1,0:T(1,128)} %near_ref.1, s32[1,1152]{1,0:T(1,128)} %mask_ref.1, f32[1,1152]{1,0:T(1,128)} %envelope_ref.1, bf16[25,13,1152]{2,1,0:T(8,128)(2,1)} %bitcast.11, f32[8,8]{1,0:T(8,128)} %mix_ref.1, ...), custom_call_target="tpu_custom_call" | custom-call | tf_op jit(solution)/shard_map/edge_convolution/pallas_call | solution.py:570
  64.6 1.5 %copy.11 = bf16[1,16,25,128]{3,1,2,0:T(8,128)(2,1)} copy(bf16[1,16,25,128]{3,1,2,0:T(8,128)(2,1)} %bitcast.12) | data formatting | bytes 204800

commit v3 on v2

--- a/solution.py
+++ b/solution.py
@@ -277,7 +277,12 @@
 
             @pl.when(t == tile)
             def _():
-                first_leg(j) if name == "leg" else merge(j)
+                if name == "leg":
+                    first_leg(j)
+                else:
+                    merge_on(is_inner, j)
+                    if j >= 1:
+                        merge_on(is_end, j - 1)
 
         return carry
 
@@ -416,6 +421,11 @@
 
         for step in range(1, peers):
             map_copy(step, j).start()
+
+    def merge_on(flag, j):
+        @pl.when(flag)
+        def _():
+            merge(j)
 
     def wait_maps(j):
         for step in range(1, peers):
@@ -483,6 +493,7 @@
         for place, (name, j) in enumerate(order[:-late])
     ]
     lax.fori_loop(0, tiles, rotate_tile, 0)
+    merge_on(is_end, pieces - late - 1)
     merge(pieces - 2)
     apply_zero()
     merge(pieces - 1)

time: 66.4 us -> 66.3 us (level)
  no operation moved by 1% of the time
where the time goes in v3:
time: 66.3 us; the launch traced here: 66.2 us
  Pallas kernels  64.6 us (97%)
  local copies, waits for them, and re-layouts  1.54 us (2%)
    pallas_call x1, Pallas kernels, shards(): pl.pallas_call(functools.partial(kernel, chips, peers), out_shape=jax.Sha...  64.6 us
    unnamed x1, local copies, waits for them, and re-layouts  1.54 us

profile of v3, /device:TPU:0, one launch (start us, length us, event | category | flops | bytes accessed | tf_op | source)
XLA Modules:
  0.0 66.2 jit_solution(153903561741021799)
XLA Ops:
  0.0 64.6 %edge_convolution.1 = bf16[25,16,128]{2,1,0:T(8,128)(2,1)} custom-call(bf16[25,16,128]{2,1,0:T(8,128)(2,1)} %bitcast.15, s32[1,64]{1,0:T(1,128)} %slot_ref.1, s32[1,1152]{1,0:T(1,128)} %near_ref.1, s32[1,1152]{1,0:T(1,128)} %mask_ref.1, f32[1,1152]{1,0:T(1,128)} %envelope_ref.1, bf16[25,13,1152]{2,1,0:T(8,128)(2,1)} %bitcast.11, f32[8,8]{1,0:T(8,128)} %mix_ref.1, ...), custom_call_target="tpu_custom_call" | custom-call | tf_op jit(solution)/shard_map/edge_convolution/pallas_call | solution.py:581
  64.6 1.5 %copy.11 = bf16[1,16,25,128]{3,1,2,0:T(8,128)(2,1)} copy(bf16[1,16,25,128]{3,1,2,0:T(8,128)(2,1)} %bitcast.12) | data formatting | bytes 204800
